TPU v7x, 128 devices: a whole 4x4x4 slice. The times are simulated.
128 devices in a mesh: feat: 4 (over z), trainer: 32 (over x, y, core).
Axes of the slice: x: 4, y: 4, z: 4, core: 2. Of those that a mesh axis runs over, the one named last changes fastest.
Arguments:
- features: bfloat16 [128, 131072], P('feat', 'trainer'), may hold values from -6 to 6
- first_adjacent: int32 [65536, 15], P('trainer'), may hold values from 0 to 4095
- first_center: int32 [65536], P('trainer'), may hold values from 0 to 4095
- first_count: int32 [65536], P('trainer'), may hold values from 1 to 15
- owner_map: int32 [65536], P('trainer'), may hold values from 0 to 127, as said below
- first_root: bfloat16 [128, 1024], P('feat'), may hold values from -0.5 to 0.5
- first_near: bfloat16 [128, 1024], P('feat'), may hold values from -0.5 to 0.5
- first_bias: float32 [1024], replicated, may hold values from -3 to 3
- second_adjacent: int32 [65536, 10], P(('feat', 'trainer')), may hold values from 0 to 1023, as said below
- second_center: int32 [65536], P(('feat', 'trainer')), may hold values from 0 to 1023, as said below
- second_count: int32 [65536], P(('feat', 'trainer')), may hold values from 1 to 10
- second_root: bfloat16 [1024, 1024], replicated, may hold values from -0.1875 to 0.1875
- second_near: bfloat16 [1024, 1024], replicated, may hold values from -0.1875 to 0.1875
- second_bias: float32 [1024], replicated, may hold values from -3 to 3
- upstream: bfloat16 [65536, 1024], P(('feat', 'trainer')), may hold values from -0.0234375 to 0.0234375
Outputs:
- layer_output: bfloat16 [65536, 1024], P(('feat', 'trainer'))
- rootgrad_two: float32 [1024, 1024], replicated
- neargrad_two: float32 [1024, 1024], replicated
- biasgrad_two: float32 [1024], replicated
- rootgrad_one: float32 [128, 1024], P('feat')
- neargrad_one: float32 [128, 1024], P('feat')
- biasgrad_one: float32 [1024], replicated
Inputs may be any that keep to these rules, and one draw needn't show every extreme that they name: `owner_map`: among the 2048 layer-one nodes of one trainer block at most 32 name any one owner; in every draw some owner is named by exactly 32 nodes of every block, and every owner is named by some node. `second_adjacent`: every entry names a filled row of the owner's table: row s * 32 + c with c smaller than the number of nodes of block s that name this owner. `second_center`: every entry names a filled row of the owner's table, as for second_adjacent.
All inputs are finite; a program needn't handle non-finite values.
Results may differ from a plain program's by a relative error of at most 0.025.
Values may be sent and summed in bfloat16 or wider, within the bound.
No kernel may reach another device: no remote copies, remote signals or barrier semaphores. Data moves between devices by JAX's collectives and lax.ppermute only.
A program may use at most 128 MiB of HBM per device.

v0:
```python
import jax
import jax.numpy as jnp
from jax import lax
from jax.sharding import PartitionSpec as P

CAP = 32


def in_one_piece(arrays, axis, dim, along):
    widths = [a.shape[along] for a in arrays]
    both = jnp.concatenate(arrays, axis=along)
    out = lax.all_gather(both, axis, axis=dim, tiled=True)
    return tuple(jnp.split(out, [sum(widths[:k]) for k in range(1, len(widths))], axis=along))


def in_one(arrays, axis):
    vector, at, finished = (jnp.concatenate([a.reshape(-1) for a in arrays]), 0, [])
    subtotal = lax.psum(vector, axis)
    for a in arrays:
        finished.append(subtotal[at : at + a.size].reshape(a.shape))
        at += a.size
    return tuple(finished)


def cross_rows(left, right):
    return lax.dot_general(
        left, right, (((0,), (0,)), ((), ())), preferred_element_type=jnp.float32
    )


def cross_cols(left, right):
    return lax.dot_general(
        left, right, (((1,), (1,)), ((), ())), preferred_element_type=jnp.float32
    )


def local(
    features,
    first_adjacent,
    first_center,
    first_count,
    owner_map,
    first_root,
    first_near,
    first_bias,
    second_adjacent,
    second_center,
    second_count,
    second_root,
    second_near,
    second_bias,
    upstream,
):
    feat_size = lax.axis_size("feat")
    trainers = lax.axis_size("trainer")
    owners_all = feat_size * trainers
    node_count = owner_map.shape[0]
    hidden_width = first_root.shape[1]
    block_width = features.shape[0]
    input_count = features.shape[1]
    fanout = first_adjacent.shape[1]
    slot_total = owners_all * CAP
    slots = trainers * CAP
    onehot = (owner_map[:, None] == jnp.arange(owners_all, dtype=jnp.int32)[None, :]).astype(
        jnp.int32
    )
    slot_rank = jnp.sum((jnp.cumsum(onehot, axis=0) - onehot) * onehot, axis=1)
    slot_node = (
        jnp.full((slot_total,), node_count, jnp.int32)
        .at[owner_map * CAP + slot_rank]
        .set(jnp.arange(node_count, dtype=jnp.int32))
    )
    filled = slot_node < node_count
    slot_adjacent = jnp.take(first_adjacent, slot_node, axis=0, mode="clip")
    slot_own = jnp.take(first_center, slot_node, axis=0, mode="clip")
    slot_count = jnp.where(filled, jnp.take(first_count, slot_node, axis=0, mode="clip"), 1)
    block_size = 512
    block_total = slot_total // block_size
    input_ids = jnp.arange(input_count, dtype=jnp.int32)[:, None]

    def select_block(pieces):
        adjacent_block, own_block, count_block, filled_block = pieces
        multiples = jnp.zeros((input_count, block_size), jnp.float32)
        for column in range(fanout):
            hits = (input_ids == adjacent_block[None, :, column]) & (
                (column < count_block) & filled_block
            )[None, :]
            multiples = multiples + jnp.where(hits, jnp.float32(1.0), jnp.float32(0.0))
        own_pick = ((input_ids == own_block[None, :]) & filled_block[None, :]).astype(jnp.bfloat16)
        own_cols = jnp.dot(features, own_pick, preferred_element_type=jnp.float32).astype(
            jnp.bfloat16
        )
        near_sum = jnp.dot(
            features, multiples.astype(jnp.bfloat16), preferred_element_type=jnp.float32
        )
        near_cols = (near_sum / count_block.astype(jnp.float32)[None, :]).astype(jnp.bfloat16)
        return (own_cols, near_cols)

    blocks_in = (
        slot_adjacent.reshape(block_total, block_size, fanout),
        slot_own.reshape(block_total, block_size),
        slot_count.reshape(block_total, block_size),
        filled.reshape(block_total, block_size),
    )
    own_blocks, near_blocks = lax.map(select_block, blocks_in)
    slot_center = own_blocks.transpose(1, 0, 2).reshape(block_width, slot_total)
    slot_near = near_blocks.transpose(1, 0, 2).reshape(block_width, slot_total)
    packed = jnp.stack([slot_center, slot_near]).reshape(2, block_width, owners_all, CAP)
    arrived = lax.all_to_all(packed, ("feat", "trainer"), split_axis=2, concat_axis=2, tiled=True)
    arrived = (
        arrived.reshape(2, block_width, feat_size, trainers, CAP)
        .transpose(0, 2, 1, 3, 4)
        .reshape(2, feat_size * block_width, slots)
    )
    owner_center = arrived[0]
    owner_near = arrived[1]
    root_all, near_all = in_one_piece((first_root, first_near), "feat", 0, 1)
    pre_one = jnp.zeros((slots, hidden_width), jnp.float32) + first_bias
    for quarter in range(feat_size):
        low = quarter * block_width
        high = low + block_width
        part = cross_rows(owner_center[low:high], root_all[low:high]) + cross_rows(
            owner_near[low:high], near_all[low:high]
        )
        pre_one = pre_one + part.astype(jnp.bfloat16).astype(jnp.float32)
    hidden_table = jax.nn.softplus(pre_one).astype(jnp.bfloat16)
    slot_ids = jnp.arange(slots, dtype=jnp.int32)
    root_pick = (second_center[:, None] == slot_ids[None, :]).astype(jnp.bfloat16)
    root_rows = jnp.dot(root_pick, hidden_table, preferred_element_type=jnp.float32).astype(
        jnp.bfloat16
    )
    multiples = jnp.zeros((second_center.shape[0], slots), jnp.float32)
    for column in range(second_adjacent.shape[1]):
        hits = (column < second_count)[:, None] & (
            second_adjacent[:, column : column + 1] == slot_ids[None, :]
        )
        multiples = multiples + jnp.where(hits, jnp.float32(1.0), jnp.float32(0.0))
    multiples = multiples.astype(jnp.bfloat16)
    divisor = second_count.astype(jnp.float32)[:, None]
    near_two = (
        jnp.dot(multiples, hidden_table, preferred_element_type=jnp.float32) / divisor
    ).astype(jnp.bfloat16)
    pre_two = jnp.dot(root_rows, second_root, preferred_element_type=jnp.float32)
    pre_two = (
        pre_two + jnp.dot(near_two, second_near, preferred_element_type=jnp.float32) + second_bias
    )
    gate = jax.nn.sigmoid(pre_two)
    layer_output = (pre_two * gate).astype(jnp.bfloat16)
    slope_two = (upstream.astype(jnp.float32) * gate * (1.0 + pre_two * (1.0 - gate))).astype(
        jnp.bfloat16
    )
    rootgrad_two, neargrad_two, biasgrad_two = lax.psum(
        (
            cross_rows(root_rows, slope_two),
            cross_rows(near_two, slope_two),
            jnp.sum(slope_two.astype(jnp.float32), axis=0),
        ),
        ("feat", "trainer"),
    )
    back_root = cross_cols(slope_two, second_root).astype(jnp.bfloat16)
    back_near = (cross_cols(slope_two, second_near) / divisor).astype(jnp.bfloat16)
    table_grad = cross_rows(root_pick, back_root) + cross_rows(multiples, back_near)
    pre_grad = (table_grad * (1.0 - jnp.exp(-hidden_table.astype(jnp.float32)))).astype(
        jnp.bfloat16
    )
    root_full = jnp.dot(owner_center, pre_grad, preferred_element_type=jnp.float32)
    near_full = jnp.dot(owner_near, pre_grad, preferred_element_type=jnp.float32)
    bias_full = jnp.sum(pre_grad.astype(jnp.float32), axis=0)
    root_sum, near_sum, biasgrad_one = in_one(
        (root_full, near_full, bias_full), ("feat", "trainer")
    )
    offset = lax.axis_index("feat") * block_width
    rootgrad_one = lax.dynamic_slice_in_dim(root_sum, offset, block_width, 0)
    neargrad_one = lax.dynamic_slice_in_dim(near_sum, offset, block_width, 0)
    return (
        layer_output,
        rootgrad_two,
        neargrad_two,
        biasgrad_two,
        rootgrad_one,
        neargrad_one,
        biasgrad_one,
    )


def solution(mesh):
    return jax.shard_map(
        local,
        mesh=mesh,
        in_specs=(
            P("feat", "trainer"),
            P("trainer", None),
            P("trainer"),
            P("trainer"),
            P("trainer"),
            P("feat", None),
            P("feat", None),
            P(),
            P(("feat", "trainer"), None),
            P(("feat", "trainer")),
            P(("feat", "trainer")),
            P(),
            P(),
            P(),
            P(("feat", "trainer"), None),
        ),
        out_specs=(
            P(("feat", "trainer"), None),
            P(),
            P(),
            P(),
            P("feat", None),
            P("feat", None),
            P(),
        ),
        check_vma=False,
    )
```

profile of v0, /device:TPU:1, one launch (start us, length us, event | category | flops | bytes accessed | tf_op | source)
XLA Modules:
  0.0 660.4 jit_solution(13970809639460819845)
XLA Ops:
  9.9 8.1 %scatter_custom_fusion = s32[4096]{0:T(1024)S(1)} fusion(s32[2048]{0:T(1024)S(1)} %compare_select_fusion.1, s32[2048]{0:T(1024)S(1)} %iota.50, s32[]{:T(128)} %constant.15.clone.1), kind=kCustom, calls=%fused_computation.160 | custom fusion | bytes 16388 | tf_op jit(solution)/shard_map/scatter | solution.py:71
  18.0 23.0 %gather_fusion.2 = s32[4096]{0:T(1024)S(1)} fusion(s32[2048]{0:T(1024)S(1)} %copy-done.1, s32[4096]{0:T(1024)S(1)} %broadcast_clamp_fusion), kind=kCustom, calls=%fused_computation.2 | custom fusion | bytes 49152 | tf_op jit(solution)/shard_map/jit(_take)/gather | solution.py:76
  41.5 14.2 %gather_fusion.1 = s32[4096,15]{1,0:T(8,128)} fusion(s32[2048,15]{1,0:T(8,128)S(1)} %copy.43, s32[4096]{0:T(1024)S(1)} %broadcast_clamp_fusion), kind=kCustom, calls=%fused_computation.1 | custom fusion | bytes 507904 | tf_op jit(solution)/shard_map/jit(_take)/gather | solution.py:74
  55.7 2.2 copy.44
  57.9 23.0 %gather_fusion = s32[4096]{0:T(1024)S(1)} fusion(s32[2048]{0:T(1024)S(1)} %copy-done.2, s32[4096]{0:T(1024)S(1)} %broadcast_clamp_fusion), kind=kCustom, calls=%fused_computation | custom fusion | bytes 49152 | tf_op jit(solution)/shard_map/jit(_take)/gather | solution.py:75
  81.0 254.4 %while.14 = (s32[]{:T(128)}, bf16[8,32,512]{2,1,0:T(8,128)(2,1)}, bf16[8,32,512]{2,1,0:T(8,128)(2,1)}, s32[8,512]{1,0:T(8,128)S(1)}, pred[8,512]{1,0:T(8,128)(4,...) while((s32[]{:T(128)}, bf16[8,32,512]{2,1,0:T(8,128)(2,1)}, ...), condition=%wide.region_5.6_spmd.clone.clone, body=%wide.region_4.5_spmd.clone.clone.sunk | while | flops 398523904 | bytes 777833 | solution.py:105
  81.5 27.7 %fusion.138 = bf16[8,32,512]{2,1,0:T(8,128)(2,1)} fusion(bf16[8,32,512]{2,1,0:T(8,128)(2,1)} %get-tuple-element.410, s32[]{:T(128)} %get-tuple-element.408, bf16[32,4096]{1,0:T(8,128)(2,1)S(1)} %get-tuple-element.422, s32[512]{0:T(512)S(1)} %bitcast.172, s32[512]{0:T(512)S(1)} %bitcast.173, s32[512]{0:T(512)S(1)} %bitcast.174, ...), kind=kOutput, calls=%fused_computation.63.clone.1 | convolution fusion | flops 260079616 | bytes 335872 | tf_op jit(solution)/shard_map/while/body/eval_jaxpr/dot_general | solution.py:93
  109.2 2.3 fusion.136
  111.7 27.7 %fusion.138 = bf16[8,32,512]{2,1,0:T(8,128)(2,1)} fusion(bf16[8,32,512]{2,1,0:T(8,128)(2,1)} %get-tuple-element.410, s32[]{:T(128)} %get-tuple-element.408, bf16[32,4096]{1,0:T(8,128)(2,1)S(1)} %get-tuple-element.422, s32[512]{0:T(512)S(1)} %bitcast.172, s32[512]{0:T(512)S(1)} %bitcast.173, s32[512]{0:T(512)S(1)} %bitcast.174, ...), kind=kOutput, calls=%fused_computation.63.clone.1 | convolution fusion | flops 260079616 | bytes 335872 | tf_op jit(solution)/shard_map/while/body/eval_jaxpr/dot_general | solution.py:93
  139.4 2.3 fusion.136
  141.9 27.7 %fusion.138 = bf16[8,32,512]{2,1,0:T(8,128)(2,1)} fusion(bf16[8,32,512]{2,1,0:T(8,128)(2,1)} %get-tuple-element.410, s32[]{:T(128)} %get-tuple-element.408, bf16[32,4096]{1,0:T(8,128)(2,1)S(1)} %get-tuple-element.422, s32[512]{0:T(512)S(1)} %bitcast.172, s32[512]{0:T(512)S(1)} %bitcast.173, s32[512]{0:T(512)S(1)} %bitcast.174, ...), kind=kOutput, calls=%fused_computation.63.clone.1 | convolution fusion | flops 260079616 | bytes 335872 | tf_op jit(solution)/shard_map/while/body/eval_jaxpr/dot_general | solution.py:93
  169.6 2.3 fusion.136
  172.1 27.7 %fusion.138 = bf16[8,32,512]{2,1,0:T(8,128)(2,1)} fusion(bf16[8,32,512]{2,1,0:T(8,128)(2,1)} %get-tuple-element.410, s32[]{:T(128)} %get-tuple-element.408, bf16[32,4096]{1,0:T(8,128)(2,1)S(1)} %get-tuple-element.422, s32[512]{0:T(512)S(1)} %bitcast.172, s32[512]{0:T(512)S(1)} %bitcast.173, s32[512]{0:T(512)S(1)} %bitcast.174, ...), kind=kOutput, calls=%fused_computation.63.clone.1 | convolution fusion | flops 260079616 | bytes 335872 | tf_op jit(solution)/shard_map/while/body/eval_jaxpr/dot_general | solution.py:93
  199.8 2.3 fusion.136
  202.3 27.7 %fusion.138 = bf16[8,32,512]{2,1,0:T(8,128)(2,1)} fusion(bf16[8,32,512]{2,1,0:T(8,128)(2,1)} %get-tuple-element.410, s32[]{:T(128)} %get-tuple-element.408, bf16[32,4096]{1,0:T(8,128)(2,1)S(1)} %get-tuple-element.422, s32[512]{0:T(512)S(1)} %bitcast.172, s32[512]{0:T(512)S(1)} %bitcast.173, s32[512]{0:T(512)S(1)} %bitcast.174, ...), kind=kOutput, calls=%fused_computation.63.clone.1 | convolution fusion | flops 260079616 | bytes 335872 | tf_op jit(solution)/shard_map/while/body/eval_jaxpr/dot_general | solution.py:93
  230.0 2.3 fusion.136
  232.4 27.7 %fusion.138 = bf16[8,32,512]{2,1,0:T(8,128)(2,1)} fusion(bf16[8,32,512]{2,1,0:T(8,128)(2,1)} %get-tuple-element.410, s32[]{:T(128)} %get-tuple-element.408, bf16[32,4096]{1,0:T(8,128)(2,1)S(1)} %get-tuple-element.422, s32[512]{0:T(512)S(1)} %bitcast.172, s32[512]{0:T(512)S(1)} %bitcast.173, s32[512]{0:T(512)S(1)} %bitcast.174, ...), kind=kOutput, calls=%fused_computation.63.clone.1 | convolution fusion | flops 260079616 | bytes 335872 | tf_op jit(solution)/shard_map/while/body/eval_jaxpr/dot_general | solution.py:93
  260.1 2.3 fusion.136
  262.6 27.7 %fusion.138 = bf16[8,32,512]{2,1,0:T(8,128)(2,1)} fusion(bf16[8,32,512]{2,1,0:T(8,128)(2,1)} %get-tuple-element.410, s32[]{:T(128)} %get-tuple-element.408, bf16[32,4096]{1,0:T(8,128)(2,1)S(1)} %get-tuple-element.422, s32[512]{0:T(512)S(1)} %bitcast.172, s32[512]{0:T(512)S(1)} %bitcast.173, s32[512]{0:T(512)S(1)} %bitcast.174, ...), kind=kOutput, calls=%fused_computation.63.clone.1 | convolution fusion | flops 260079616 | bytes 335872 | tf_op jit(solution)/shard_map/while/body/eval_jaxpr/dot_general | solution.py:93
  290.3 2.3 fusion.136
  292.8 27.7 %fusion.138 = bf16[8,32,512]{2,1,0:T(8,128)(2,1)} fusion(bf16[8,32,512]{2,1,0:T(8,128)(2,1)} %get-tuple-element.410, s32[]{:T(128)} %get-tuple-element.408, bf16[32,4096]{1,0:T(8,128)(2,1)S(1)} %get-tuple-element.422, s32[512]{0:T(512)S(1)} %bitcast.172, s32[512]{0:T(512)S(1)} %bitcast.173, s32[512]{0:T(512)S(1)} %bitcast.174, ...), kind=kOutput, calls=%fused_computation.63.clone.1 | convolution fusion | flops 260079616 | bytes 335872 | tf_op jit(solution)/shard_map/while/body/eval_jaxpr/dot_general | solution.py:93
  320.5 2.3 fusion.136
  341.5 2.7 copy.54
  344.1 4.5 reshape.178
  348.6 11.5 %all-to-all-start = ((bf16[128,2,1024]{2,1,0:T(2,128)(2,1)}), bf16[128,2,1024]{2,1,0:T(2,128)(2,1)S(1)}, u32[]{:S(2)}, u32[]{:S(2)}) async-start(bf16[128,2,1024]{2,1,0:T(2,128)(2,1)} %reshape.178), calls=%async_computation | async-start | bytes 1048576 | tf_op jit(solution)/shard_map/all_to_all | solution.py:109
  360.2 15.7 %all_gather.3 = bf16[128,2048]{1,0:T(8,128)(2,1)} all-gather(bf16[32,2048]{1,0:T(8,128)(2,1)S(1)} %pad_maximum_fusion.2), channel_id=1, replica_groups=mesh['feat'=4,'trainer'=32] {'feat'}, dimensions={0}, use_global_device_ids=true | all-gather | bytes 655360 | tf_op jit(solution)/shard_map/all_gather | solution.py:12
  377.7 2.0 reshape.179
  379.7 2.9 copy.53
  388.0 1.9 slice.221
  389.8 3.5 fusion.81
  393.4 3.6 fusion.78
  400.0 3.6 fusion.75
  407.4 3.6 fusion.84
  411.9 3.1 add_convert_fusion.12
  419.8 4.4 fusion.53
  428.2 7.0 %divide_convert_fusion.1 = bf16[512,1024]{1,0:T(8,128)(2,1)S(1)} fusion(bf16[1024,1024]{1,0:T(8,128)(2,1)S(1)} %fusion.53, f32[512]{0:T(512)S(1)} %copy-done.27, s32[512]{0:T(512)S(1)} %bitcast.204, s32[512]{0:T(512)S(1)} %bitcast.206, s32[512]{0:T(512)S(1)} %bitcast.190, s32[512]{0:T(512)S(1)} %bitcast.192, s32[512]{0:T(512)S(1)} %bitcast.194, ...), kind=kOutput, calls=%fused_computation.101 | convolution fusion | flops 1095761920 | bytes 3173376 | tf_op jit(solution)/shard_map/dot_general | solution.py:141
  435.3 3.5 convert_reduce_fusion.1
  438.7 6.2 fusion.54
  444.9 5.0 fusion.96
  449.9 3.3 fusion.95
  453.3 11.6 %convert_reduce_fusion = (f32[1024]{0:T(1024)S(1)}, bf16[1024,1024]{1,0:T(8,128)(2,1)}) fusion(bf16[1024,1024]{1,0:T(8,128)(2,1)} %copy-done.44, f32[1024,1024]{1,0:T(8,128)} %fusion.54, bf16[512,1024]{1,0:T(8,128)(2,1)} %get-tuple-element.226, bf16[1024,1024]{1,0:T(8,128)(2,1)S(1)} %copy-done, f32[512]{0:T(512)S(1)} %copy-done.27, s32[512]{0:T(512)S(1)} %bitcast.205, ...), kind=kOutput, calls=%fused_computation.87 | convolution fusion | flops 2177891328 | bytes 11566080 | tf_op jit(solution)/shard_map/dot_general | solution.py:26
  464.8 2.3 squeeze.13
  467.2 2.0 convolution_bitcast_fusion.1
  471.2 2.1 convolution_bitcast_fusion
  474.5 67.6 %psum.30 = f32[1024]{0:T(1024)} all-reduce(f32[1024]{0:T(1024)S(1)} %get-tuple-element.225), channel_id=1, replica_groups=mesh['feat'=4,'trainer'=32] {'feat','trainer'}, use_global_device_ids=true, to_apply=%region_9.10 | all-reduce | flops 1024 | bytes 8192 | tf_op jit(solution)/shard_map/psum | solution.py:152
  542.1 99.2 %all-reduce.3.cloned.1.call-done = (f32[1024,1024]{1,0:T(8,128)}, f32[1024,1024]{1,0:T(8,128)}, f32[263168]{0:T(1024)}) async-done(((f32[1024,1024]{1,0:T(8,128)}, f32[1024,1024]{1,0:T(8,128)}, f32[263168]{0:T(1024)}), (f32[1024,1024]{1,0:T(8,128)}, f32[1024,1024]{1,0:T(8,128)}, f32[263168]{0:T(1024)})) %all-reduce.3.cloned.1.call-update) | async-done | bytes 9441296 | tf_op jit(solution)/shard_map/psum | solution.py:152
  646.5 4.9 copy.69
  651.4 2.0 copy.70
  (174 shorter events, 42.0 us)
Async XLA Ops:
  7.2 428.1 %copy-start = (bf16[1024,1024]{1,0:T(8,128)(2,1)S(1)}, bf16[1024,1024]{1,0:T(8,128)(2,1)}, u32[]{:S(2)}) copy-start(bf16[1024,1024]{1,0:T(8,128)(2,1)} %param.29) | copy-start | bytes 6291460
  8.5 0.7 copy-start.15
  8.6 9.3 %copy-start.1 = (s32[2048]{0:T(1024)S(1)}, s32[2048]{0:T(1024)}, u32[]{:S(2)}) copy-start(s32[2048]{0:T(1024)} %param.20) | copy-start | bytes 24580
  18.0 23.1 %copy-start.14 = (s32[2048,15]{0,1:T(8,128)S(1)}, s32[2048,15]{0,1:T(8,128)}, u32[]{:S(2)}) copy-start(s32[2048,15]{0,1:T(8,128)} %param.18) | copy-start | bytes 368644
  55.7 2.2 copy-start.2
  57.9 23.1 %copy-start.40 = (bf16[32,4096]{1,0:T(8,128)(2,1)S(1)}, bf16[32,4096]{1,0:T(8,128)(2,1)}, u32[]{:S(2)}) copy-start(bf16[32,4096]{1,0:T(8,128)(2,1)} %param.17) | copy-start | bytes 786436
  344.1 16.0 %copy-start.17 = (bf16[32,1024]{1,0:T(8,128)(2,1)S(1)}, bf16[32,1024]{1,0:T(8,128)(2,1)}, u32[]{:S(2)}) copy-start(bf16[32,1024]{1,0:T(8,128)(2,1)} %param.23) | copy-start | bytes 196612
  344.1 16.0 %copy-start.18 = (bf16[32,1024]{1,0:T(8,128)(2,1)S(1)}, bf16[32,1024]{1,0:T(8,128)(2,1)}, u32[]{:S(2)}) copy-start(bf16[32,1024]{1,0:T(8,128)(2,1)} %param.22) | copy-start | bytes 196612
  344.1 31.8 %copy-start.20 = (s32[512]{0:T(512)S(1)}, s32[512]{0:T(512)}, u32[]{:S(2)}) copy-start(s32[512]{0:T(512)} %param.27) | copy-start | bytes 6148
  344.1 33.0 %copy-start.19 = (s32[512,10]{0,1:T(8,128)S(1)}, s32[512,10]{0,1:T(8,128)}, u32[]{:S(2)}) copy-start(s32[512,10]{0,1:T(8,128)} %param.25) | copy-start | bytes 61444
  348.6 29.1 %all-to-all-start = ((bf16[128,2,1024]{2,1,0:T(2,128)(2,1)}), bf16[128,2,1024]{2,1,0:T(2,128)(2,1)S(1)}, u32[]{:S(2)}, u32[]{:S(2)}) async-start(bf16[128,2,1024]{2,1,0:T(2,128)(2,1)} %reshape.178), calls=%async_computation | async-start | bytes 1048576 | tf_op jit(solution)/shard_map/all_to_all | solution.py:109
  360.1 281.2 %all-reduce.3.cloned.1.call-start = ((), (), s32[]{:S(2)}) async-start(), calls=%async_computation.1 | async-start | bytes 18882560 | tf_op jit(solution)/shard_map/psum | solution.py:152
  389.8 3.5 copy-start.13
  411.9 3.5 copy-start.3
  415.3 2.2 copy-start.4
  415.3 2.2 copy-start.12
  417.6 2.2 copy-start.6
  417.6 2.2 copy-start.16
  417.6 2.2 copy-start.41
  419.8 4.4 copy-start.43
  424.2 3.8 copy-start.44
  424.2 2.4 copy-start.38
  426.6 1.4 copy-start.9
  426.6 1.4 copy-start.21
  426.6 1.4 copy-start.22
  426.6 1.5 copy-start.23
  426.6 1.5 copy-start.24
  426.6 1.5 copy-start.25
  426.6 1.5 copy-start.26
  426.6 1.5 copy-start.27
  426.6 1.5 copy-start.28
  426.6 1.5 copy-start.29
  426.6 1.5 copy-start.30
  426.6 1.5 copy-start.31
  426.7 1.5 copy-start.32
  426.7 1.5 copy-start.33
  426.7 1.5 copy-start.34
  426.7 1.5 copy-start.35
  426.7 1.5 copy-start.36
  426.7 1.5 copy-start.37
  428.2 7.1 %copy-start.39 = (bf16[512,1024]{1,0:T(8,128)(2,1)S(1)}, bf16[512,1024]{1,0:T(8,128)(2,1)}, u32[]{:S(2)}) copy-start(bf16[512,1024]{1,0:T(8,128)(2,1)} %param.31) | copy-start | bytes 3145732
  428.2 7.1 %copy-start.42 = (f32[1024]{0:T(1024)S(1)}, f32[1024]{0:T(1024)}, u32[]{:S(2)}) copy-start(f32[1024]{0:T(1024)} %param.30) | copy-start | bytes 12292
  435.2 3.5 copy-start.11
  444.9 5.0 copy-start.7
  444.9 5.0 copy-start.10
  471.2 2.2 copy-start.8
  646.5 4.9 copy-start.5
Sparse Core Ops, SparseCore 0:
  474.6 166.6 all-reduce.2
where the time goes:
time: 665 us; the launch traced here: 660 us
  matrix products  309 us (46%)
  local copies, waits for them, and re-layouts  123 us (18%)
  waiting for transfers between devices  99.2 us (15%)
  blocking collectives  83.4 us (13%)
  between operations  15 us (2%)
  loops' own time  13.2 us (2%)
  starting transfers between devices  11.5 us (2%)
    dot_general x8, matrix products, select_block(): jnp.dot(features, multiples.astype(jnp.bfloat16), preferred_element_type=...  222 us
    psum x1, waiting for transfers between devices, local(): lax.psum((cross_rows(root_rows, slope_two), cross_rows(near_two, slope_tw...  99.2 us
    psum x1, blocking collectives, local(): lax.psum((cross_rows(root_rows, slope_two), cross_rows(near_two, slope_tw...  67.6 us
    dot_general x12, matrix products, cross_rows(): lax.dot_general(left, right, (((0,), (0,)), ((), ())), preferred_element_...  51.3 us
    gather x1, local copies, waits for them, and re-layouts, local(): slot_own = jnp.take(first_center, slot_node, axis=0, mode='clip')  23 us
    gather x1, local copies, waits for them, and re-layouts, local(): jnp.take(first_count, slot_node, axis=0, mode='clip')  23 us
    unnamed x98, local copies, waits for them, and re-layouts  19.4 us
    dot_general x8, matrix products, select_block(): jnp.dot(features, own_pick, preferred_element_type=jnp.float32)  18.4 us
  transfers between devices with their start and end apart: 2, of which 1 were waited for; matrix products, arithmetic and copies ran while one was open for 0% of the time, Pallas kernels for 0%

commit v1 on v0

--- a/solution.py
+++ b/solution.py
@@ -149,13 +149,20 @@
     slope_two = (upstream.astype(jnp.float32) * gate * (1.0 + pre_two * (1.0 - gate))).astype(
         jnp.bfloat16
     )
-    rootgrad_two, neargrad_two, biasgrad_two = lax.psum(
+
+    def resolve_the_sizes(frame, axis_tag, named_axis):
+        for s in (axis_tag, named_axis):
+            frame = lax.psum(frame, s)
+        return frame
+
+    rootgrad_two, neargrad_two, biasgrad_two = resolve_the_sizes(
         (
             cross_rows(root_rows, slope_two),
             cross_rows(near_two, slope_two),
             jnp.sum(slope_two.astype(jnp.float32), axis=0),
         ),
-        ("feat", "trainer"),
+        "trainer",
+        "feat",
     )
     back_root = cross_cols(slope_two, second_root).astype(jnp.bfloat16)
     back_near = (cross_cols(slope_two, second_near) / divisor).astype(jnp.bfloat16)

time: 665 us -> 909 us (1.37)
  waiting for transfers between devices: 99.2 us -> 345 us
    psum x1 -> x3, waiting for transfers between devices: 99.2 us -> 345 us  [the longest x2 265 us: resolve_the_sizes(): frame = lax.psum(frame, s)]
    psum x1 -> x2, blocking collectives: 67.6 us -> 72.4 us  [resolve_the_sizes(): frame = lax.psum(frame, s)]
    unnamed x98 -> x96, local copies, waits for them, and re-layouts: 19.4 us -> 21.5 us
  transfers between devices with their start and end apart: 2 -> 4, of which waited for: 1 -> 3; matrix products, arithmetic and copies ran while one was open for 0% -> 2% of each run, Pallas kernels for 0% -> 0%
where the time goes in v1:
time: 909 us; the launch traced here: 905 us
  waiting for transfers between devices  345 us (38%)
  matrix products  303 us (33%)
  local copies, waits for them, and re-layouts  124 us (14%)
  blocking collectives  87.7 us (10%)
  between operations  14.7 us (2%)
  loops' own time  13.2 us (1%)
  starting transfers between devices  11.6 us (1%)
    psum x2, waiting for transfers between devices, resolve_the_sizes(): frame = lax.psum(frame, s)  265 us
    dot_general x8, matrix products, select_block(): jnp.dot(features, multiples.astype(jnp.bfloat16), preferred_element_type=...  222 us
    psum x1, waiting for transfers between devices, in_one(): subtotal = lax.psum(vector, axis)  80.4 us
    psum x2, blocking collectives, resolve_the_sizes(): frame = lax.psum(frame, s)  72.4 us
    dot_general x12, matrix products, cross_rows(): lax.dot_general(left, right, (((0,), (0,)), ((), ())), preferred_element_...  44.8 us
    gather x1, local copies, waits for them, and re-layouts, local(): slot_own = jnp.take(first_center, slot_node, axis=0, mode='clip')  23 us
    gather x1, local copies, waits for them, and re-layouts, local(): jnp.take(first_count, slot_node, axis=0, mode='clip')  23 us
    unnamed x96, local copies, waits for them, and re-layouts  21.5 us
  transfers between devices with their start and end apart: 4, of which 3 were waited for; matrix products, arithmetic and copies ran while one was open for 2% of the time, Pallas kernels for 0%

profile of v1, /device:TPU:1, one launch (start us, length us, event | category | flops | bytes accessed | tf_op | source)
XLA Modules:
  0.0 905.0 jit_solution(2341747962652245053)
XLA Ops:
  9.9 8.1 scatter_custom_fusion
  18.0 23.0 %gather_fusion.2 = s32[4096]{0:T(1024)S(1)} fusion(s32[2048]{0:T(1024)S(1)} %copy-done.1, s32[4096]{0:T(1024)S(1)} %broadcast_clamp_fusion), kind=kCustom, calls=%fused_computation.2 | custom fusion | bytes 49152 | tf_op jit(solution)/shard_map/jit(_take)/gather | solution.py:76
  41.5 14.2 %gather_fusion.1 = s32[4096,15]{1,0:T(8,128)} fusion(s32[2048,15]{1,0:T(8,128)S(1)} %copy.43, s32[4096]{0:T(1024)S(1)} %broadcast_clamp_fusion), kind=kCustom, calls=%fused_computation.1 | custom fusion | bytes 507904 | tf_op jit(solution)/shard_map/jit(_take)/gather | solution.py:74
  55.7 2.2 copy.44
  57.9 23.0 %gather_fusion = s32[4096]{0:T(1024)S(1)} fusion(s32[2048]{0:T(1024)S(1)} %copy-done.2, s32[4096]{0:T(1024)S(1)} %broadcast_clamp_fusion), kind=kCustom, calls=%fused_computation | custom fusion | bytes 49152 | tf_op jit(solution)/shard_map/jit(_take)/gather | solution.py:75
  81.0 254.4 %while.14 = (s32[]{:T(128)}, bf16[8,32,512]{2,1,0:T(8,128)(2,1)}, bf16[8,32,512]{2,1,0:T(8,128)(2,1)}, s32[8,512]{1,0:T(8,128)S(1)}, pred[8,512]{1,0:T(8,128)(4,...) while((s32[]{:T(128)}, bf16[8,32,512]{2,1,0:T(8,128)(2,1)}, ...), condition=%wide.region_5.6_spmd.clone.clone, body=%wide.region_4.5_spmd.clone.clone.sunk | while | flops 398523904 | bytes 777833 | solution.py:105
  81.5 27.7 %fusion.138 = bf16[8,32,512]{2,1,0:T(8,128)(2,1)} fusion(bf16[8,32,512]{2,1,0:T(8,128)(2,1)} %get-tuple-element.411, s32[]{:T(128)} %get-tuple-element.409, bf16[32,4096]{1,0:T(8,128)(2,1)S(1)} %get-tuple-element.423, s32[512]{0:T(512)S(1)} %bitcast.172, s32[512]{0:T(512)S(1)} %bitcast.173, s32[512]{0:T(512)S(1)} %bitcast.174, ...), kind=kOutput, calls=%fused_computation.63.clone.1 | convolution fusion | flops 260079616 | bytes 335872 | tf_op jit(solution)/shard_map/while/body/eval_jaxpr/dot_general | solution.py:93
  109.2 2.3 fusion.136
  111.7 27.7 %fusion.138 = bf16[8,32,512]{2,1,0:T(8,128)(2,1)} fusion(bf16[8,32,512]{2,1,0:T(8,128)(2,1)} %get-tuple-element.411, s32[]{:T(128)} %get-tuple-element.409, bf16[32,4096]{1,0:T(8,128)(2,1)S(1)} %get-tuple-element.423, s32[512]{0:T(512)S(1)} %bitcast.172, s32[512]{0:T(512)S(1)} %bitcast.173, s32[512]{0:T(512)S(1)} %bitcast.174, ...), kind=kOutput, calls=%fused_computation.63.clone.1 | convolution fusion | flops 260079616 | bytes 335872 | tf_op jit(solution)/shard_map/while/body/eval_jaxpr/dot_general | solution.py:93
  139.4 2.3 fusion.136
  141.9 27.7 %fusion.138 = bf16[8,32,512]{2,1,0:T(8,128)(2,1)} fusion(bf16[8,32,512]{2,1,0:T(8,128)(2,1)} %get-tuple-element.411, s32[]{:T(128)} %get-tuple-element.409, bf16[32,4096]{1,0:T(8,128)(2,1)S(1)} %get-tuple-element.423, s32[512]{0:T(512)S(1)} %bitcast.172, s32[512]{0:T(512)S(1)} %bitcast.173, s32[512]{0:T(512)S(1)} %bitcast.174, ...), kind=kOutput, calls=%fused_computation.63.clone.1 | convolution fusion | flops 260079616 | bytes 335872 | tf_op jit(solution)/shard_map/while/body/eval_jaxpr/dot_general | solution.py:93
  169.6 2.3 fusion.136
  172.1 27.7 %fusion.138 = bf16[8,32,512]{2,1,0:T(8,128)(2,1)} fusion(bf16[8,32,512]{2,1,0:T(8,128)(2,1)} %get-tuple-element.411, s32[]{:T(128)} %get-tuple-element.409, bf16[32,4096]{1,0:T(8,128)(2,1)S(1)} %get-tuple-element.423, s32[512]{0:T(512)S(1)} %bitcast.172, s32[512]{0:T(512)S(1)} %bitcast.173, s32[512]{0:T(512)S(1)} %bitcast.174, ...), kind=kOutput, calls=%fused_computation.63.clone.1 | convolution fusion | flops 260079616 | bytes 335872 | tf_op jit(solution)/shard_map/while/body/eval_jaxpr/dot_general | solution.py:93
  199.8 2.3 fusion.136
  202.3 27.7 %fusion.138 = bf16[8,32,512]{2,1,0:T(8,128)(2,1)} fusion(bf16[8,32,512]{2,1,0:T(8,128)(2,1)} %get-tuple-element.411, s32[]{:T(128)} %get-tuple-element.409, bf16[32,4096]{1,0:T(8,128)(2,1)S(1)} %get-tuple-element.423, s32[512]{0:T(512)S(1)} %bitcast.172, s32[512]{0:T(512)S(1)} %bitcast.173, s32[512]{0:T(512)S(1)} %bitcast.174, ...), kind=kOutput, calls=%fused_computation.63.clone.1 | convolution fusion | flops 260079616 | bytes 335872 | tf_op jit(solution)/shard_map/while/body/eval_jaxpr/dot_general | solution.py:93
  230.0 2.3 fusion.136
  232.4 27.7 %fusion.138 = bf16[8,32,512]{2,1,0:T(8,128)(2,1)} fusion(bf16[8,32,512]{2,1,0:T(8,128)(2,1)} %get-tuple-element.411, s32[]{:T(128)} %get-tuple-element.409, bf16[32,4096]{1,0:T(8,128)(2,1)S(1)} %get-tuple-element.423, s32[512]{0:T(512)S(1)} %bitcast.172, s32[512]{0:T(512)S(1)} %bitcast.173, s32[512]{0:T(512)S(1)} %bitcast.174, ...), kind=kOutput, calls=%fused_computation.63.clone.1 | convolution fusion | flops 260079616 | bytes 335872 | tf_op jit(solution)/shard_map/while/body/eval_jaxpr/dot_general | solution.py:93
  260.1 2.3 fusion.136
  262.6 27.7 %fusion.138 = bf16[8,32,512]{2,1,0:T(8,128)(2,1)} fusion(bf16[8,32,512]{2,1,0:T(8,128)(2,1)} %get-tuple-element.411, s32[]{:T(128)} %get-tuple-element.409, bf16[32,4096]{1,0:T(8,128)(2,1)S(1)} %get-tuple-element.423, s32[512]{0:T(512)S(1)} %bitcast.172, s32[512]{0:T(512)S(1)} %bitcast.173, s32[512]{0:T(512)S(1)} %bitcast.174, ...), kind=kOutput, calls=%fused_computation.63.clone.1 | convolution fusion | flops 260079616 | bytes 335872 | tf_op jit(solution)/shard_map/while/body/eval_jaxpr/dot_general | solution.py:93
  290.3 2.3 fusion.136
  292.8 27.7 %fusion.138 = bf16[8,32,512]{2,1,0:T(8,128)(2,1)} fusion(bf16[8,32,512]{2,1,0:T(8,128)(2,1)} %get-tuple-element.411, s32[]{:T(128)} %get-tuple-element.409, bf16[32,4096]{1,0:T(8,128)(2,1)S(1)} %get-tuple-element.423, s32[512]{0:T(512)S(1)} %bitcast.172, s32[512]{0:T(512)S(1)} %bitcast.173, s32[512]{0:T(512)S(1)} %bitcast.174, ...), kind=kOutput, calls=%fused_computation.63.clone.1 | convolution fusion | flops 260079616 | bytes 335872 | tf_op jit(solution)/shard_map/while/body/eval_jaxpr/dot_general | solution.py:93
  320.5 2.3 fusion.136
  341.5 2.7 copy.54
  344.1 4.5 reshape.178
  348.6 11.5 %all-to-all-start = ((bf16[128,2,1024]{2,1,0:T(2,128)(2,1)}), bf16[128,2,1024]{2,1,0:T(2,128)(2,1)S(1)}, u32[]{:S(2)}, u32[]{:S(2)}) async-start(bf16[128,2,1024]{2,1,0:T(2,128)(2,1)} %reshape.178), calls=%async_computation | async-start | bytes 1048576 | tf_op jit(solution)/shard_map/all_to_all | solution.py:109
  360.2 15.3 %all_gather.3 = bf16[128,2048]{1,0:T(8,128)(2,1)S(1)} all-gather(bf16[32,2048]{1,0:T(8,128)(2,1)S(1)} %pad_maximum_fusion.2), channel_id=1, replica_groups=mesh['feat'=4,'trainer'=32] {'feat'}, dimensions={0}, use_global_device_ids=true | all-gather | bytes 655360 | tf_op jit(solution)/shard_map/all_gather | solution.py:12
  379.3 2.9 copy.53
  388.4 2.7 fusion.81
  391.0 2.7 fusion.78
  396.9 3.6 fusion.75
  401.7 2.7 fusion.84
  404.7 3.1 add_convert_fusion.12
  412.5 3.5 fusion.53
  420.0 7.0 divide_convert_fusion.1
  427.1 3.1 convert_reduce_fusion.1
  430.2 5.9 fusion.54
  436.1 4.6 fusion.96
  440.7 3.3 fusion.95
  444.0 11.3 %convert_reduce_fusion = (f32[1024]{0:T(1024)S(1)}, bf16[1024,1024]{1,0:T(8,128)(2,1)}) fusion(bf16[1024,1024]{1,0:T(8,128)(2,1)} %copy-done.43, f32[1024,1024]{1,0:T(8,128)} %fusion.54, bf16[512,1024]{1,0:T(8,128)(2,1)S(1)} %get-tuple-element.227, bf16[1024,1024]{1,0:T(8,128)(2,1)S(1)} %copy-done, f32[512]{0:T(512)S(1)} %copy-done.26, ...), kind=kOutput, calls=%fused_computation.87 | convolution fusion | flops 2177891328 | bytes 11566080 | tf_op jit(solution)/shard_map/dot_general | solution.py:26
  455.4 3.0 fusion.90
  458.4 2.3 squeeze.13
  464.8 2.7 convolution_bitcast_fusion
  468.8 108.3 %all-reduce.8.cloned.1.call-done = (f32[1024,1024]{1,0:T(8,128)}, f32[1024,1024]{1,0:T(8,128)}) async-done(((f32[1024,1024]{1,0:T(8,128)}, f32[1024,1024]{1,0:T(8,128)}), (f32[1024,1024]{1,0:T(8,128)}, f32[1024,1024]{1,0:T(8,128)})) %all-reduce.8.cloned.1.call-update) | async-done | bytes 8388624 | tf_op jit(solution)/shard_map/psum | solution.py:155
  577.1 62.9 %psum.53 = f32[1024]{0:T(1024)S(1)} all-reduce(f32[1024]{0:T(1024)S(1)} %get-tuple-element.226), channel_id=1, replica_groups=mesh['feat'=4,'trainer'=32] {'trainer'}, use_global_device_ids=true, to_apply=%region_11.12 | all-reduce | flops 1024 | bytes 8192 | tf_op jit(solution)/shard_map/psum | solution.py:155
  640.0 9.5 %psum.54 = f32[1024]{0:T(1024)} all-reduce(f32[1024]{0:T(1024)S(1)} %psum.53), channel_id=1, replica_groups=mesh['feat'=4,'trainer'=32] {'feat'}, use_global_device_ids=true, to_apply=%region_12.13 | all-reduce | flops 1024 | bytes 8192 | tf_op jit(solution)/shard_map/psum | solution.py:155
  649.5 80.4 %all-reduce.6.cloned.1.call-done = f32[263168]{0:T(1024)} async-done(((f32[263168]{0:T(1024)}), f32[263168]{0:T(1024)}) %all-reduce.6.cloned.1.call-update) | async-done | bytes 1052688 | tf_op jit(solution)/shard_map/psum | solution.py:18
  735.0 156.3 %all-reduce.10.cloned.1.call-done = (f32[1024,1024]{1,0:T(8,128)}, f32[1024,1024]{1,0:T(8,128)}) async-done(((f32[1024,1024]{1,0:T(8,128)}, f32[1024,1024]{1,0:T(8,128)}), (f32[1024,1024]{1,0:T(8,128)}, f32[1024,1024]{1,0:T(8,128)})) %all-reduce.10.cloned.1.call-update) | async-done | bytes 8388624 | tf_op jit(solution)/shard_map/psum | solution.py:155
  891.4 4.9 copy.71
  (179 shorter events, 45.9 us)
Async XLA Ops:
  7.2 419.9 %copy-start = (bf16[1024,1024]{1,0:T(8,128)(2,1)S(1)}, bf16[1024,1024]{1,0:T(8,128)(2,1)}, u32[]{:S(2)}) copy-start(bf16[1024,1024]{1,0:T(8,128)(2,1)} %param.29) | copy-start | bytes 6291460
  8.5 0.7 copy-start.15
  8.6 9.3 %copy-start.1 = (s32[2048]{0:T(1024)S(1)}, s32[2048]{0:T(1024)}, u32[]{:S(2)}) copy-start(s32[2048]{0:T(1024)} %param.20) | copy-start | bytes 24580
  18.0 23.1 %copy-start.14 = (s32[2048,15]{0,1:T(8,128)S(1)}, s32[2048,15]{0,1:T(8,128)}, u32[]{:S(2)}) copy-start(s32[2048,15]{0,1:T(8,128)} %param.18) | copy-start | bytes 368644
  55.7 2.2 copy-start.2
  57.9 23.1 %copy-start.39 = (bf16[32,4096]{1,0:T(8,128)(2,1)S(1)}, bf16[32,4096]{1,0:T(8,128)(2,1)}, u32[]{:S(2)}) copy-start(bf16[32,4096]{1,0:T(8,128)(2,1)} %param.17) | copy-start | bytes 786436
  344.1 16.0 %copy-start.16 = (bf16[32,1024]{1,0:T(8,128)(2,1)S(1)}, bf16[32,1024]{1,0:T(8,128)(2,1)}, u32[]{:S(2)}) copy-start(bf16[32,1024]{1,0:T(8,128)(2,1)} %param.23) | copy-start | bytes 196612
  344.1 16.0 %copy-start.17 = (bf16[32,1024]{1,0:T(8,128)(2,1)S(1)}, bf16[32,1024]{1,0:T(8,128)(2,1)}, u32[]{:S(2)}) copy-start(bf16[32,1024]{1,0:T(8,128)(2,1)} %param.22) | copy-start | bytes 196612
  344.1 31.3 %copy-start.19 = (s32[512]{0:T(512)S(1)}, s32[512]{0:T(512)}, u32[]{:S(2)}) copy-start(s32[512]{0:T(512)} %param.27) | copy-start | bytes 6148
  344.1 32.5 %copy-start.18 = (s32[512,10]{0,1:T(8,128)S(1)}, s32[512,10]{0,1:T(8,128)}, u32[]{:S(2)}) copy-start(s32[512,10]{0,1:T(8,128)} %param.25) | copy-start | bytes 61444
  348.6 28.7 %all-to-all-start = ((bf16[128,2,1024]{2,1,0:T(2,128)(2,1)}), bf16[128,2,1024]{2,1,0:T(2,128)(2,1)S(1)}, u32[]{:S(2)}, u32[]{:S(2)}) async-start(bf16[128,2,1024]{2,1,0:T(2,128)(2,1)} %reshape.178), calls=%async_computation | async-start | bytes 1048576 | tf_op jit(solution)/shard_map/all_to_all | solution.py:109
  360.1 216.9 %all-reduce.8.cloned.1.call-start = ((), (), s32[]{:S(2)}) async-start(), calls=%async_computation.2 | async-start | bytes 16777216 | tf_op jit(solution)/shard_map/psum | solution.py:155
  382.2 1.8 copy-start.3
  388.4 2.7 copy-start.13
  404.6 3.5 copy-start.4
  408.1 2.2 copy-start.5
  408.1 2.2 copy-start.12
  410.3 2.2 copy-start.7
  410.3 2.2 copy-start.40
  412.5 3.5 copy-start.42
  416.0 3.8 copy-start.43
  416.0 2.4 copy-start.37
  418.4 1.4 copy-start.9
  418.4 1.4 copy-start.20
  418.4 1.4 copy-start.21
  418.4 1.5 copy-start.22
  418.4 1.5 copy-start.23
  418.4 1.5 copy-start.24
  418.4 1.5 copy-start.25
  418.4 1.5 copy-start.26
  418.5 1.5 copy-start.27
  418.5 1.5 copy-start.28
  418.5 1.5 copy-start.29
  418.5 1.5 copy-start.30
  418.5 1.5 copy-start.31
  418.5 1.5 copy-start.32
  418.5 1.5 copy-start.33
  418.5 1.5 copy-start.34
  418.5 1.5 copy-start.35
  418.5 1.5 copy-start.36
  420.0 7.1 copy-start.38
  420.0 7.1 copy-start.41
  427.1 3.1 copy-start.11
  436.1 4.6 copy-start.10
  455.3 274.6 %all-reduce.6.cloned.1.call-start = ((), (), s32[]{:S(2)}) async-start(), calls=%async_computation.1 | async-start | bytes 2105344 | tf_op jit(solution)/shard_map/psum | solution.py:18
  464.8 2.8 copy-start.8
  468.7 422.7 %all-reduce.10.cloned.1.call-start = ((), (), s32[]{:S(2)}) async-start(), calls=%async_computation.3 | async-start | bytes 16777216 | tf_op jit(solution)/shard_map/psum | solution.py:155
  891.4 4.9 copy-start.6
Sparse Core Ops, SparseCore 0:
  455.4 121.5 all-reduce.7
  581.8 148.0 all-reduce.5
  732.5 158.8 all-reduce.9
